TPU v7x, 32 devices: a whole 2x2x4 slice. The times are simulated.
32 devices in a mesh: dp: 4 (over y, x), sp: 8 (over z, core).
Axes of the slice: x: 2, y: 2, z: 4, core: 2. Of those that a mesh axis runs over, the one named last changes fastest.
Arguments:
- first_layer_input: bfloat16 [8, 1024, 1024], P('dp', 'sp'), may hold values from -6 to 6
- cotangent: bfloat16 [8, 1024, 1024], P('dp', 'sp'), may hold values from -6 to 6
- document_begin: int32 [8, 1024], P('dp'), may hold values from 0 to 1023, as said below
- query_key_value_weight: bfloat16 [2, 1024, 3072], P(None, 'dp'), may hold values from -0.1875 to 0.1875
- attention_out_weight: bfloat16 [2, 1024, 1024], P(None, 'dp'), may hold values from -0.5 to 0.5
- feedforward_in_weight: bfloat16 [2, 1024, 4096], P(None, 'dp'), may hold values from -0.1875 to 0.1875
- feedforward_out_weight: bfloat16 [2, 4096, 1024], P(None, 'dp'), may hold values from -0.09375 to 0.09375
- query_value_bias: float32 [2, 2, 1024], replicated, may hold values from -3 to 3
- attention_out_bias: float32 [2, 1024], replicated, may hold values from -2 to 2
- feedforward_in_bias: float32 [2, 4096], replicated, may hold values from -2 to 2
- feedforward_out_bias: float32 [2, 1024], replicated, may hold values from -2 to 2
- layernorm_gain: float32 [2, 2, 1024], replicated, may hold values from 0.25 to 1.75
- layernorm_bias: float32 [2, 2, 1024], replicated, may hold values from -2 to 2
- adapter_down_maps: float32 [2, 2, 4, 1024], replicated, may hold values from -0.1875 to 0.1875
- adapter_up_maps: float32 [2, 2, 4, 1024], replicated, may hold values from -0.3 to 0.3
Outputs:
- output: float32 [8, 1024, 1024], P('dp', 'sp')
- input_grad: float32 [8, 1024, 1024], P('dp', 'sp')
- grad_down: float32 [2, 2, 4, 1024], replicated
- grad_up: float32 [2, 2, 4, 1024], replicated
Inputs may be any that keep to these rules, and one draw needn't show every extreme that they name: document_begin[s, t] is the first position of the document that holds token t of slot s: 0 at t = 0, never falling along a slot, equal to t where a document begins and constant inside a document. Of every aligned group of 2 slots, one is a single document; in every other slot the last token is a document of its own.
All inputs are finite; a program needn't handle non-finite values.
Results may differ from a plain program's by a relative error of at most 0.014.
Values may be sent and summed in bfloat16 or wider, within the bound.
A program may use at most 192 MiB of HBM per device.

v0:
```python
from functools import partial
import math
import jax
import jax.numpy as jnp
from jax import lax
from jax.sharding import PartitionSpec as P

HEAD_SIZE = 64
EPSILON = 1e-05
ADAPTER_ALPHA = 32.0
EXACT_PRECISION = lax.Precision.HIGHEST
MASKED = -1e30


def layer_norm(tensor, gains, shifts):
    row_mean = jnp.mean(tensor, -1, keepdims=True)
    centred = tensor - row_mean
    spread = jnp.mean(centred * centred, -1, keepdims=True)
    return centred * lax.rsqrt(spread + EPSILON) * gains + shifts


def fetch_weights(
    query_key_value_weight,
    attention_out_weight,
    feedforward_in_weight,
    feedforward_out_weight,
    layer_number,
):
    return (
        lax.all_gather(query_key_value_weight[layer_number], "dp", axis=0, tiled=True),
        lax.all_gather(attention_out_weight[layer_number], "dp", axis=0, tiled=True),
        lax.all_gather(feedforward_in_weight[layer_number], "dp", axis=0, tiled=True),
        lax.all_gather(feedforward_out_weight[layer_number], "dp", axis=0, tiled=True),
    )


def sum_adapters(down_terms, up_terms):
    return lax.psum((down_terms, up_terms), ("dp", "sp"))


def slot_scores(query_rows, key_rows, document_starts):
    length = query_rows.shape[0]
    heads_q = query_rows.reshape(length, -1, HEAD_SIZE)
    heads_k = key_rows.reshape(length, -1, HEAD_SIZE)
    scores = jnp.einsum("qhd,khd->hqk", heads_q, heads_k, preferred_element_type=jnp.float32)
    places = jnp.arange(length)
    allowed = (document_starts[:, None] == document_starts[None, :]) & (
        places[None, :] <= places[:, None]
    )
    return jnp.where(allowed[None], scores, MASKED)


def slot_forward(slot_items):
    query_rows, key_rows, value_rows, document_starts = slot_items
    length = query_rows.shape[0]
    scores = slot_scores(query_rows, key_rows, document_starts)
    row_max = jnp.max(scores, -1, keepdims=True)
    row_total = jnp.sum(jnp.exp(scores - row_max), -1, keepdims=True)
    log_total = row_max + jnp.log(row_total)
    probability = jnp.exp(scores - log_total).astype(jnp.bfloat16)
    mixture = jnp.einsum(
        "hqk,khd->qhd",
        probability,
        value_rows.reshape(length, -1, HEAD_SIZE),
        preferred_element_type=jnp.float32,
    )
    return (mixture.reshape(length, -1).astype(jnp.bfloat16), log_total[..., 0])


def slot_backward(slot_items):
    query_rows, key_rows, value_rows, document_starts, log_total, grad_mixture = slot_items
    length = query_rows.shape[0]
    scores = slot_scores(query_rows, key_rows, document_starts)
    probability = jnp.exp(scores - log_total[..., None])
    low_probability = probability.astype(jnp.bfloat16)
    grad_heads = grad_mixture.reshape(length, -1, HEAD_SIZE)
    value_heads = value_rows.reshape(length, -1, HEAD_SIZE)
    grad_values = jnp.einsum(
        "hqk,qhd->khd", low_probability, grad_heads, preferred_element_type=jnp.float32
    )
    grad_prob = jnp.einsum(
        "qhd,khd->hqk", grad_heads, value_heads, preferred_element_type=jnp.float32
    )
    grad_scores = probability * (grad_prob - jnp.sum(probability * grad_prob, -1, keepdims=True))
    low_scores = grad_scores.astype(jnp.bfloat16)
    grad_queries = jnp.einsum(
        "hqk,khd->qhd",
        low_scores,
        key_rows.reshape(length, -1, HEAD_SIZE),
        preferred_element_type=jnp.float32,
    )
    grad_keys = jnp.einsum(
        "hqk,qhd->khd",
        low_scores,
        query_rows.reshape(length, -1, HEAD_SIZE),
        preferred_element_type=jnp.float32,
    )
    return (
        grad_queries.reshape(length, -1).astype(jnp.bfloat16),
        grad_keys.reshape(length, -1).astype(jnp.bfloat16),
        grad_values.reshape(length, -1).astype(jnp.bfloat16),
    )


def layer_forward(hidden_state, weight_set, params, document_begin):
    query_key_value_weight, attention_out_weight, feedforward_in_weight, feedforward_out_weight = (
        weight_set
    )
    (
        query_value_bias,
        attention_out_bias,
        feedforward_in_bias,
        feedforward_out_bias,
        gains,
        shifts,
        down_projection,
        up_projection,
    ) = params
    model_dimension = hidden_state.shape[-1]
    normed = layer_norm(hidden_state, gains[0], shifts[0]).astype(jnp.bfloat16)
    projected_rows = jnp.einsum(
        "std,de->ste", normed, query_key_value_weight, preferred_element_type=jnp.float32
    )
    widened = normed.astype(jnp.float32)
    adapter_scale = ADAPTER_ALPHA / down_projection.shape[1]
    query_row_block = jnp.einsum(
        "nyh,lh->nyl", widened, down_projection[0], precision=EXACT_PRECISION
    )
    value_row_block = jnp.einsum(
        "nyh,lh->nyl", widened, down_projection[1], precision=EXACT_PRECISION
    )
    query_rows = (
        (
            projected_rows[..., :model_dimension]
            + query_value_bias[0]
            + adapter_scale
            * jnp.einsum(
                "wah,hp->wap", query_row_block, up_projection[0], precision=EXACT_PRECISION
            )
        )
        * HEAD_SIZE ** (-0.5)
    ).astype(jnp.bfloat16)
    key_rows = projected_rows[..., model_dimension : 2 * model_dimension].astype(jnp.bfloat16)
    value_rows = (
        projected_rows[..., 2 * model_dimension :]
        + query_value_bias[1]
        + adapter_scale
        * jnp.einsum("wah,hp->wap", value_row_block, up_projection[1], precision=EXACT_PRECISION)
    ).astype(jnp.bfloat16)
    queries_h, keys_h, values_h = (
        lax.all_to_all(query_rows, "sp", split_axis=2, concat_axis=1, tiled=True),
        lax.all_to_all(key_rows, "sp", split_axis=2, concat_axis=1, tiled=True),
        lax.all_to_all(value_rows, "sp", split_axis=2, concat_axis=1, tiled=True),
    )
    mixture_h, log_total = lax.map(slot_forward, (queries_h, keys_h, values_h, document_begin))
    mixture = lax.all_to_all(mixture_h, "sp", split_axis=1, concat_axis=2, tiled=True)
    attended = hidden_state + (
        jnp.einsum("std,de->ste", mixture, attention_out_weight, preferred_element_type=jnp.float32)
        + attention_out_bias
    )
    normed_mlp = layer_norm(attended, gains[1], shifts[1]).astype(jnp.bfloat16)
    pre_act = (
        jnp.einsum(
            "std,df->stf", normed_mlp, feedforward_in_weight, preferred_element_type=jnp.float32
        )
        + feedforward_in_bias
    )
    activation = jax.nn.gelu(pre_act, approximate=True).astype(jnp.bfloat16)
    final_result = attended + (
        jnp.einsum(
            "stf,fd->std", activation, feedforward_out_weight, preferred_element_type=jnp.float32
        )
        + feedforward_out_bias
    )
    saved_state = (
        normed,
        query_row_block,
        value_row_block,
        queries_h,
        keys_h,
        values_h,
        log_total,
        attended,
        pre_act,
    )
    return (final_result, saved_state)


def layer_backward(hidden_state, gradient, weight_set, params, document_begin, saved_state):
    query_key_value_weight, attention_out_weight, feedforward_in_weight, feedforward_out_weight = (
        weight_set
    )
    (
        query_value_bias,
        attention_out_bias,
        feedforward_in_bias,
        feedforward_out_bias,
        gains,
        shifts,
        down_projection,
        up_projection,
    ) = params
    (
        normed,
        query_row_block,
        value_row_block,
        queries_h,
        keys_h,
        values_h,
        log_total,
        attended,
        pre_act,
    ) = saved_state
    grad_act = jnp.einsum(
        "std,fd->stf",
        gradient.astype(jnp.bfloat16),
        feedforward_out_weight,
        preferred_element_type=jnp.float32,
    )
    unused_act, gelu_back = jax.vjp(partial(jax.nn.gelu, approximate=True), pre_act)
    grad_pre = gelu_back(grad_act)[0].astype(jnp.bfloat16)
    grad_normed_mlp = jnp.einsum(
        "stf,df->std", grad_pre, feedforward_in_weight, preferred_element_type=jnp.float32
    )
    unused_norm, second_back = jax.vjp(
        lambda tensor: layer_norm(tensor, gains[1], shifts[1]), attended
    )
    grad_attended = gradient + second_back(grad_normed_mlp)[0]
    grad_mixture = jnp.einsum(
        "ste,de->std",
        grad_attended.astype(jnp.bfloat16),
        attention_out_weight,
        preferred_element_type=jnp.float32,
    ).astype(jnp.bfloat16)
    grad_mixture_h = lax.all_to_all(grad_mixture, "sp", split_axis=2, concat_axis=1, tiled=True)
    grad_q_h, grad_k_h, grad_v_h = lax.map(
        slot_backward, (queries_h, keys_h, values_h, document_begin, log_total, grad_mixture_h)
    )
    grad_queries, grad_keys, grad_values = (
        lax.all_to_all(grad_q_h, "sp", split_axis=1, concat_axis=2, tiled=True),
        lax.all_to_all(grad_k_h, "sp", split_axis=1, concat_axis=2, tiled=True),
        lax.all_to_all(grad_v_h, "sp", split_axis=1, concat_axis=2, tiled=True),
    )
    grad_queries = grad_queries * jnp.asarray(HEAD_SIZE ** (-0.5), jnp.bfloat16)
    stacked = jnp.concatenate([grad_queries, grad_keys, grad_values], -1)
    grad_normed = jnp.einsum(
        "ste,de->std", stacked, query_key_value_weight, preferred_element_type=jnp.float32
    )
    adapter_scale = ADAPTER_ALPHA / down_projection.shape[1]
    widened = normed.astype(jnp.float32)
    query_widened = grad_queries.astype(jnp.float32)
    value_widened = grad_values.astype(jnp.float32)
    query_row_gradient = adapter_scale * jnp.einsum(
        "nyh,lh->nyl", query_widened, up_projection[0], precision=EXACT_PRECISION
    )
    value_row_gradient = adapter_scale * jnp.einsum(
        "nyh,lh->nyl", value_widened, up_projection[1], precision=EXACT_PRECISION
    )
    query_up_weight = adapter_scale * jnp.einsum(
        "fkp,fkz->pz", query_row_block, query_widened, precision=EXACT_PRECISION
    )
    value_up_weight = adapter_scale * jnp.einsum(
        "fkp,fkz->pz", value_row_block, value_widened, precision=EXACT_PRECISION
    )
    down_q = jnp.einsum("fkp,fkz->pz", query_row_gradient, widened, precision=EXACT_PRECISION)
    down_v = jnp.einsum("fkp,fkz->pz", value_row_gradient, widened, precision=EXACT_PRECISION)
    grad_normed = (
        grad_normed
        + jnp.einsum(
            "wah,hp->wap", query_row_gradient, down_projection[0], precision=EXACT_PRECISION
        )
        + jnp.einsum(
            "wah,hp->wap", value_row_gradient, down_projection[1], precision=EXACT_PRECISION
        )
    )
    unused_first, first_back = jax.vjp(
        lambda tensor: layer_norm(tensor, gains[0], shifts[0]), hidden_state
    )
    grad_hidden = grad_attended + first_back(grad_normed)[0]
    return (grad_hidden, jnp.stack([down_q, down_v]), jnp.stack([query_up_weight, value_up_weight]))


def body(
    first_layer_input,
    cotangent,
    document_begin,
    query_key_value_weight,
    attention_out_weight,
    feedforward_in_weight,
    feedforward_out_weight,
    query_value_bias,
    attention_out_bias,
    feedforward_in_bias,
    feedforward_out_bias,
    layernorm_gain,
    layernorm_bias,
    adapter_down_maps,
    adapter_up_maps,
):
    layers = query_key_value_weight.shape[0]

    def params_of(layer_number):
        return (
            query_value_bias[layer_number],
            attention_out_bias[layer_number],
            feedforward_in_bias[layer_number],
            feedforward_out_bias[layer_number],
            layernorm_gain[layer_number],
            layernorm_bias[layer_number],
            adapter_down_maps[layer_number],
            adapter_up_maps[layer_number],
        )

    hidden_state = first_layer_input.astype(jnp.float32)
    inputs = []
    gathered = []
    for layer_number in range(layers):
        weight_set = fetch_weights(
            query_key_value_weight,
            attention_out_weight,
            feedforward_in_weight,
            feedforward_out_weight,
            layer_number,
        )
        inputs.append(hidden_state)
        gathered.append(weight_set)
        hidden_state, unused_state = layer_forward(
            hidden_state, weight_set, params_of(layer_number), document_begin
        )
    gradient = cotangent.astype(jnp.float32)
    down_parts = [None] * layers
    up_parts = [None] * layers
    for layer_number in reversed(range(layers)):
        weight_set = fetch_weights(
            query_key_value_weight,
            attention_out_weight,
            feedforward_in_weight,
            feedforward_out_weight,
            layer_number,
        )
        unused_result, saved_state = layer_forward(
            inputs[layer_number], weight_set, params_of(layer_number), document_begin
        )
        gradient, down_terms, up_terms = layer_backward(
            inputs[layer_number],
            gradient,
            weight_set,
            params_of(layer_number),
            document_begin,
            saved_state,
        )
        down_parts[layer_number] = down_terms
        up_parts[layer_number] = up_terms
    grad_down = jnp.stack(down_parts)
    grad_up = jnp.stack(up_parts)
    grad_down, grad_up = sum_adapters(grad_down, grad_up)
    tokens = (
        first_layer_input.shape[0]
        * first_layer_input.shape[1]
        * lax.axis_size("dp")
        * lax.axis_size("sp")
    )
    token_scale = 1.0 / math.sqrt(tokens)
    return (hidden_state, gradient, grad_down * token_scale, grad_up * token_scale)


def solution(mesh):
    placed = (
        P("dp", "sp", None),
        P("dp", "sp", None),
        P("dp", None),
        P(None, "dp", None),
        P(None, "dp", None),
        P(None, "dp", None),
        P(None, "dp", None),
        P(),
        P(),
        P(),
        P(),
        P(),
        P(),
        P(),
        P(),
    )
    return jax.shard_map(
        body,
        mesh=mesh,
        in_specs=placed,
        out_specs=(P("dp", "sp", None), P("dp", "sp", None), P(), P()),
        check_vma=False,
    )
```

profile of v0, /device:TPU:0, one launch (start us, length us, event | category | flops | bytes accessed | tf_op | source)
XLA Modules:
  0.0 1025.3 jit_solution(3215920100778661397)
XLA Ops:
  25.0 59.0 %all-gather.17.cloned.1.call-done = bf16[1,1024,3072]{2,1,0:T(8,128)(2,1)} async-done(((bf16[1,256,3072]{2,1,0:T(8,128)(2,1)}), bf16[1,1024,3072]{2,1,0:T(8,128)(2,1)}) %all-gather.17.cloned.1.call-update) | async-done | bytes 6291472 | tf_op jit(solution)/shard_map/all_gather | solution.py:30
  101.4 11.2 %all-to-all-done = bf16[2,128,1024]{1,0,2:T(2,128)(2,1)S(1)} async-done(((bf16[2,128,1024]{1,0,2:T(2,128)(2,1)}), bf16[2,128,1024]{1,0,2:T(2,128)(2,1)S(1)}, u32[]{:S(2)}, u32[]{:S(2)}) %all-to-all-start) | async-done | bytes 524320 | tf_op jit(solution)/shard_map/all_to_all | solution.py:153
  118.6 12.9 %all-to-all-done.1 = bf16[2,128,1024]{1,0,2:T(2,128)(2,1)S(1)} async-done(((bf16[2,128,1024]{1,0,2:T(2,128)(2,1)}), bf16[2,128,1024]{1,0,2:T(2,128)(2,1)S(1)}, u32[]{:S(2)}, u32[]{:S(2)}) %all-to-all-start.1) | async-done | bytes 524320 | tf_op jit(solution)/shard_map/all_to_all | solution.py:151
  136.9 13.3 %all-to-all-done.2 = bf16[2,128,1024]{1,0,2:T(2,128)(2,1)S(1)} async-done(((bf16[2,128,1024]{1,0,2:T(2,128)(2,1)}), bf16[2,128,1024]{1,0,2:T(2,128)(2,1)S(1)}, u32[]{:S(2)}, u32[]{:S(2)}) %all-to-all-start.2) | async-done | bytes 524320 | tf_op jit(solution)/shard_map/all_to_all | solution.py:152
  150.9 12.9 %while.72 = (s32[]{:T(128)}, bf16[2,1024,128]{1,2,0:T(8,128)(2,1)S(1)}, bf16[2,1024,128]{1,2,0:T(8,128)(2,1)S(1)}, s32[2,1024]{1,0:T(2,128)S(1)}, bf16[2,1024,12...) while((s32[]{:T(128)}, bf16[2,1024,128]{1,2,0:T(8,128)(2,1)S(1)}, ...), condition=%wide.region_5.6_spmd, body=%wide.region_2.5_spmd.sunk | while | flops 556922880 | bytes 32575588 | solution.py:155
  169.3 14.6 %all-to-all-done.3 = bf16[2,1024,128]{2,0,1:T(2,128)(2,1)S(1)} async-done(((bf16[2,1024,128]{2,0,1:T(2,128)(2,1)}), bf16[2,1024,128]{2,0,1:T(2,128)(2,1)S(1)}, u32[]{:S(2)}, u32[]{:S(2)}) %all-to-all-start.3) | async-done | bytes 524320 | tf_op jit(solution)/shard_map/all_to_all | solution.py:156
  188.2 22.6 %all-gather.23.cloned.1.call-done = bf16[1,4096,1024]{2,1,0:T(8,128)(2,1)} async-done(((bf16[1,1024,1024]{2,1,0:T(8,128)(2,1)}), bf16[1,4096,1024]{2,1,0:T(8,128)(2,1)}) %all-gather.23.cloned.1.call-update) | async-done | bytes 8388624 | tf_op jit(solution)/shard_map/all_gather | solution.py:33
  210.8 89.3 %all-gather.21.cloned.1.call-done = bf16[1,1024,4096]{2,1,0:T(8,128)(2,1)} async-done(((bf16[1,256,4096]{2,1,0:T(8,128)(2,1)}), bf16[1,1024,4096]{2,1,0:T(8,128)(2,1)}) %all-gather.21.cloned.1.call-update) | async-done | bytes 8388624 | tf_op jit(solution)/shard_map/all_gather | solution.py:32
  300.1 11.5 %fusion.337 = (f32[2,128]{1,0:T(2,128)S(1)}, f32[2,128,1024]{2,1,0:T(8,128)S(1)}) fusion(f32[2,128,1024]{2,1,0:T(8,128)} %copy-done.51, f32[1024]{0:T(1024)S(1)} %bitcast.735, bf16[1,4096,1024]{2,1,0:T(8,128)(2,1)} %all-gather.23.cloned.1.call-done, bf16[1,1024,4096]{2,1,0:T(8,128)(2,1)} %all-gather.21.cloned.1.call-done, f32[4096]{0:T(1024)S(1)} %bitcast.730, ...), kind=kOutput, calls=%fused_computation.425 | convolution fusion | flops 4307550208 | bytes 18906112 | tf_op jit(solution)/shard_map/stf,fd->std/dot_general | solution.py:170
  313.4 58.7 %all-gather.25.cloned.1.call-done = bf16[1,1024,3072]{2,1,0:T(8,128)(2,1)} async-done(((bf16[1,256,3072]{2,1,0:T(8,128)(2,1)}), bf16[1,1024,3072]{2,1,0:T(8,128)(2,1)}) %all-gather.25.cloned.1.call-update) | async-done | bytes 6291472 | tf_op jit(solution)/shard_map/all_gather | solution.py:30
  391.3 10.9 %all-to-all-done.4 = bf16[2,128,1024]{1,0,2:T(2,128)(2,1)} async-done(((bf16[2,128,1024]{1,0,2:T(2,128)(2,1)}), bf16[2,128,1024]{1,0,2:T(2,128)(2,1)}, u32[]{:S(2)}, u32[]{:S(2)}) %all-to-all-start.4) | async-done | bytes 524320 | tf_op jit(solution)/shard_map/all_to_all | solution.py:153
  409.8 11.2 %all-to-all-done.5 = bf16[2,128,1024]{1,0,2:T(2,128)(2,1)S(1)} async-done(((bf16[2,128,1024]{1,0,2:T(2,128)(2,1)}), bf16[2,128,1024]{1,0,2:T(2,128)(2,1)S(1)}, u32[]{:S(2)}, u32[]{:S(2)}) %all-to-all-start.5) | async-done | bytes 524320 | tf_op jit(solution)/shard_map/all_to_all | solution.py:151
  433.3 7.7 all-to-all-done.6
  446.1 16.5 %while.74 = (s32[]{:T(128)}, bf16[2,1024,128]{1,2,0:T(8,128)(2,1)}, f32[2,2,1024]{2,1,0:T(2,128)S(1)}, bf16[2,1024,128]{1,2,0:T(8,128)(2,1)S(1)}, s32[2,1024]{1,...) while((s32[]{:T(128)}, bf16[2,1024,128]{1,2,0:T(8,128)(2,1)}, ...), condition=%wide.region_19.20_spmd, body=%wide.region_16.19_spmd.sunk | while | flops 556922880 | bytes 36778152 | solution.py:155
  468.9 15.4 %all-to-all-done.8 = bf16[2,1024,128]{2,0,1:T(2,128)(2,1)} async-done(((bf16[2,1024,128]{2,0,1:T(2,128)(2,1)}), bf16[2,1024,128]{2,0,1:T(2,128)(2,1)}, u32[]{:S(2)}, u32[]{:S(2)}) %all-to-all-start.8) | async-done | bytes 524320 | tf_op jit(solution)/shard_map/all_to_all | solution.py:156
  492.3 6.6 all-gather.29.cloned.1.call-done
  498.9 8.2 fusion.75
  507.1 81.4 %all-gather.31.cloned.1.call-done = bf16[1,4096,1024]{2,1,0:T(8,128)(2,1)} async-done(((bf16[1,1024,1024]{2,1,0:T(8,128)(2,1)}), bf16[1,4096,1024]{2,1,0:T(8,128)(2,1)}) %all-gather.31.cloned.1.call-update) | async-done | bytes 8388624 | tf_op jit(solution)/shard_map/all_gather | solution.py:33
  588.5 12.2 %multiply_reduce_fusion.5 = (f32[2,128]{1,0:T(2,128)S(1)}, f32[2,128,1024]{2,1,0:T(8,128)}) fusion(f32[2,128,1024]{2,1,0:T(8,128)S(1)} %copy-done.22, f32[2,128]{1,0:T(2,128)S(1)} %broadcast_multiply_fusion.5, f32[1024]{0:T(1024)S(1)} %bitcast.744, bf16[1,1024,4096]{2,1,0:T(8,128)(2,1)} %all-gather.29.cloned.1.call-done, f32[2,128,4096]{2,1,0:T(8,128)} %fusion.75, ...), kind=kOutput, calls=%fused_computation.279 | convolution fusion | flops 4316987392 | bytes 23599104 | tf_op jit(solution)/shard_map/stf,df->std/dot_general | solution.py:222
  613.3 15.4 %while.76 = (s32[]{:T(128)}, bf16[2,1024,128]{1,2,0:T(8,128)(2,1)}, f32[2,2,1024]{2,1,0:T(2,128)}, bf16[2,1024,128]{1,2,0:T(8,128)(2,1)S(1)}, s32[2,1024]{1,0:T(...) while((s32[]{:T(128)}, bf16[2,1024,128]{1,2,0:T(8,128)(2,1)}, ...), condition=%wide.region_32.33_spmd, body=%wide.region_29.32_spmd.sunk | while | flops 556922880 | bytes 32583792 | solution.py:155
  643.3 27.2 %while.75 = (s32[]{:T(128)}, bf16[2,1024,128]{1,2,0:T(8,128)(2,1)}, bf16[2,1024,128]{1,2,0:T(8,128)(2,1)}, bf16[2,1024,128]{1,2,0:T(8,128)(2,1)}, bf16[2,1024,12...) while((s32[]{:T(128)}, bf16[2,1024,128]{1,2,0:T(8,128)(2,1)}, ...), condition=%wide.region_26.27_spmd, body=%wide.region_24.26_spmd.sunk | while | flops 1370880000 | bytes 88150360 | solution.py:236
  685.1 8.0 all-to-all-done.12
  697.2 7.8 fusion.69
  707.0 5.5 all-to-all-done.11
  716.0 12.9 %while.73 = (s32[]{:T(128)}, bf16[2,1024,128]{1,2,0:T(8,128)(2,1)S(1)}, bf16[2,1024,128]{1,2,0:T(8,128)(2,1)S(1)}, s32[2,1024]{1,0:T(2,128)S(1)}, bf16[2,1024,12...) while((s32[]{:T(128)}, bf16[2,1024,128]{1,2,0:T(8,128)(2,1)S(1)}, ...), condition=%wide.region_13.14_spmd, body=%wide.region_10.13_spmd.sunk | while | flops 556922880 | bytes 32575588 | solution.py:155
  749.0 11.9 %multiply_reduce_fusion.2 = (f32[2,128]{1,0:T(2,128)S(1)}, f32[2,128,1024]{2,1,0:T(8,128)}) fusion(f32[2,128,1024]{2,1,0:T(8,128)S(1)} %copy-done.29, f32[2,128]{1,0:T(2,128)S(1)} %broadcast_multiply_fusion.4, f32[1024]{0:T(1024)S(1)} %bitcast.748, bf16[1,1024,4096]{2,1,0:T(8,128)(2,1)} %all-gather.21.cloned.1.call-done, f32[2,128,4096]{2,1,0:T(8,128)} %fusion.69, ...), kind=kOutput, calls=%fused_computation.273 | convolution fusion | flops 4317249536 | bytes 24123392 | tf_op jit(solution)/shard_map/stf,df->std/dot_general | solution.py:222
  776.6 11.1 %all-to-all-done.14 = bf16[2,128,1024]{1,0,2:T(2,128)(2,1)S(1)} async-done(((bf16[2,128,1024]{1,0,2:T(2,128)(2,1)}), bf16[2,128,1024]{1,0,2:T(2,128)(2,1)S(1)}, u32[]{:S(2)}, u32[]{:S(2)}) %all-to-all-start.14) | async-done | bytes 524320 | tf_op jit(solution)/shard_map/all_to_all | solution.py:235
  792.7 28.4 %while.77 = (s32[]{:T(128)}, bf16[2,1024,128]{1,2,0:T(8,128)(2,1)}, bf16[2,1024,128]{1,2,0:T(8,128)(2,1)}, bf16[2,1024,128]{1,2,0:T(8,128)(2,1)}, bf16[2,1024,12...) while((s32[]{:T(128)}, bf16[2,1024,128]{1,2,0:T(8,128)(2,1)}, ...), condition=%wide.region_39.40_spmd, body=%wide.region_37.39_spmd.sunk | while | flops 1370880000 | bytes 86053176 | solution.py:236
  830.7 11.2 %all-to-all-done.17 = bf16[2,1024,128]{2,0,1:T(2,128)(2,1)S(1)} async-done(((bf16[2,1024,128]{2,0,1:T(2,128)(2,1)}), bf16[2,1024,128]{2,0,1:T(2,128)(2,1)S(1)}, u32[]{:S(2)}, u32[]{:S(2)}) %all-to-all-start.17) | async-done | bytes 524320 | tf_op jit(solution)/shard_map/all_to_all | solution.py:242
  846.5 12.0 %fusion.191 = f32[2,128,1024]{2,1,0:T(8,128)} fusion(f32[2,128,1024]{2,1,0:T(8,128)S(1)} %get-tuple-element.421, bf16[1,4096,1024]{2,1,0:T(8,128)(2,1)} %all-gather.31.cloned.1.call-done, bf16[1,1024,4096]{2,1,0:T(8,128)(2,1)} %all-gather.29.cloned.1.call-done, f32[4096]{0:T(1024)S(1)} %bitcast.729, f32[1024]{0:T(1024)S(1)} %bitcast.732, ...), kind=kOutput, calls=%fused_computation.233 | convolution fusion | flops 4307288064 | bytes 18905088 | tf_op jit(solution)/shard_map/stf,fd->std/dot_general | solution.py:170
  871.8 11.3 %all-to-all-done.16 = bf16[2,1024,128]{2,0,1:T(2,128)(2,1)S(1)} async-done(((bf16[2,1024,128]{2,0,1:T(2,128)(2,1)}), bf16[2,1024,128]{2,0,1:T(2,128)(2,1)S(1)}, u32[]{:S(2)}, u32[]{:S(2)}) %all-to-all-start.16) | async-done | bytes 524320 | tf_op jit(solution)/shard_map/all_to_all | solution.py:241
  897.1 118.2 %all-reduce.3.cloned.1.call-done = (f32[2,2,4,1024]{3,2,1,0:T(4,128)}, f32[2,2,4,1024]{3,2,1,0:T(4,128)}) async-done(((f32[2,2,4,1024]{3,2,1,0:T(4,128)}, f32[2,2,4,1024]{3,2,1,0:T(4,128)}), (f32[2,2,4,1024]{3,2,1,0:T(4,128)}, f32[2,2,4,1024]{3,2,1,0:T(4,128)})) %all-reduce.3.cloned.1.call-update) | async-done | bytes 131088 | tf_op jit(solution)/shard_map/psum | solution.py:38
  (587 shorter events, 364.5 us)
Async XLA Ops:
  7.2 76.9 %all-gather.17.cloned.1.call-start = ((), (), s32[]{:S(2)}) async-start(), calls=%async_computation.18 | async-start | bytes 7864320 | tf_op jit(solution)/shard_map/all_gather | solution.py:30
  11.0 174.3 %all-gather.19.cloned.1.call-start = ((), (), s32[]{:S(2)}) async-start(), calls=%async_computation.19 | async-start | bytes 2621440 | tf_op jit(solution)/shard_map/all_gather | solution.py:31
  12.1 198.7 %all-gather.23.cloned.1.call-start = ((), (), s32[]{:S(2)}) async-start(), calls=%async_computation.21 | async-start | bytes 10485760 | tf_op jit(solution)/shard_map/all_gather | solution.py:33
  16.8 283.3 %all-gather.21.cloned.1.call-start = ((), (), s32[]{:S(2)}) async-start(), calls=%async_computation.20 | async-start | bytes 10485760 | tf_op jit(solution)/shard_map/all_gather | solution.py:32
  21.8 350.3 %all-gather.25.cloned.1.call-start = ((), (), s32[]{:S(2)}) async-start(), calls=%async_computation.22 | async-start | bytes 7864320 | tf_op jit(solution)/shard_map/all_gather | solution.py:30
  22.4 466.1 %all-gather.27.cloned.1.call-start = ((), (), s32[]{:S(2)}) async-start(), calls=%async_computation.23 | async-start | bytes 2621440 | tf_op jit(solution)/shard_map/all_gather | solution.py:31
  22.9 476.0 %all-gather.29.cloned.1.call-start = ((), (), s32[]{:S(2)}) async-start(), calls=%async_computation.24 | async-start | bytes 10485760 | tf_op jit(solution)/shard_map/all_gather | solution.py:32
  24.2 474.7 %copy-start.106 = (f32[1,1,1024]{2,1,0:T(1,128)}, f32[1,1,1024]{2,1,0:T(1,128)S(1)}, u32[]{:S(2)}) copy-start(f32[1,1,1024]{2,1,0:T(1,128)S(1)} %get-tuple-element.404) | copy-start | bytes 12292
  24.3 288.3 %copy-start.69 = (f32[1,1,1024]{2,1,0:T(1,128)}, f32[1,1,1024]{2,1,0:T(1,128)S(1)}, u32[]{:S(2)}) copy-start(f32[1,1,1024]{2,1,0:T(1,128)S(1)} %get-tuple-element.403) | copy-start | bytes 12292
  24.3 564.2 %copy-start.108 = (f32[1,1,1024]{2,1,0:T(1,128)}, f32[1,1,1024]{2,1,0:T(1,128)S(1)}, u32[]{:S(2)}) copy-start(f32[1,1,1024]{2,1,0:T(1,128)S(1)} %get-tuple-element.400) | copy-start | bytes 12292
  92.7 20.0 %all-to-all-start = ((bf16[2,128,1024]{1,0,2:T(2,128)(2,1)}), bf16[2,128,1024]{1,0,2:T(2,128)(2,1)S(1)}, u32[]{:S(2)}, u32[]{:S(2)}) async-start(bf16[2,128,1024]{1,0,2:T(2,128)(2,1)} %copy.57), calls=%async_computation | async-start | bytes 1048576 | tf_op jit(solution)/shard_map/all_to_all | solution.py:153
  112.7 18.8 %all-to-all-start.1 = ((bf16[2,128,1024]{1,0,2:T(2,128)(2,1)}), bf16[2,128,1024]{1,0,2:T(2,128)(2,1)S(1)}, u32[]{:S(2)}, u32[]{:S(2)}) async-start(bf16[2,128,1024]{1,0,2:T(2,128)(2,1)} %copy.59), calls=%async_computation.1 | async-start | bytes 1048576 | tf_op jit(solution)/shard_map/all_to_all | solution.py:151
  131.4 18.8 %all-to-all-start.2 = ((bf16[2,128,1024]{1,0,2:T(2,128)(2,1)}), bf16[2,128,1024]{1,0,2:T(2,128)(2,1)S(1)}, u32[]{:S(2)}, u32[]{:S(2)}) async-start(bf16[2,128,1024]{1,0,2:T(2,128)(2,1)} %copy.61), calls=%async_computation.2 | async-start | bytes 1048576 | tf_op jit(solution)/shard_map/all_to_all | solution.py:152
  135.0 453.5 %all-gather.31.cloned.1.call-start = ((), (), s32[]{:S(2)}) async-start(), calls=%async_computation.25 | async-start | bytes 10485760 | tf_op jit(solution)/shard_map/all_gather | solution.py:33
  135.8 352.7 %copy-start.59 = (f32[1,1024]{1,0:T(1,128)}, f32[1,1024]{1,0:T(1,128)S(1)}, u32[]{:S(2)}) copy-start(f32[1,1024]{1,0:T(1,128)S(1)} %get-tuple-element.414) | copy-start | bytes 12292
  164.9 19.0 %all-to-all-start.3 = ((bf16[2,1024,128]{2,0,1:T(2,128)(2,1)}), bf16[2,1024,128]{2,0,1:T(2,128)(2,1)S(1)}, u32[]{:S(2)}, u32[]{:S(2)}) async-start(bf16[2,1024,128]{2,0,1:T(2,128)(2,1)} %copy.63), calls=%async_computation.3 | async-start | bytes 1048576 | tf_op jit(solution)/shard_map/all_to_all | solution.py:156
  169.3 329.6 %copy-start.87 = (f32[1,4096]{1,0:T(1,128)}, f32[1,4096]{1,0:T(1,128)S(1)}, u32[]{:S(2)}) copy-start(f32[1,4096]{1,0:T(1,128)S(1)} %get-tuple-element.398) | copy-start | bytes 49156
  382.1 20.1 %all-to-all-start.4 = ((bf16[2,128,1024]{1,0,2:T(2,128)(2,1)}), bf16[2,128,1024]{1,0,2:T(2,128)(2,1)}, u32[]{:S(2)}, u32[]{:S(2)}) async-start(bf16[2,128,1024]{1,0,2:T(2,128)(2,1)} %copy.65), calls=%async_computation.4 | async-start | bytes 1048576 | tf_op jit(solution)/shard_map/all_to_all | solution.py:153
  402.2 18.8 %all-to-all-start.5 = ((bf16[2,128,1024]{1,0,2:T(2,128)(2,1)}), bf16[2,128,1024]{1,0,2:T(2,128)(2,1)S(1)}, u32[]{:S(2)}, u32[]{:S(2)}) async-start(bf16[2,128,1024]{1,0,2:T(2,128)(2,1)} %copy.67), calls=%async_computation.5 | async-start | bytes 1048576 | tf_op jit(solution)/shard_map/all_to_all | solution.py:151
  421.0 20.0 %all-to-all-start.6 = ((bf16[2,128,1024]{1,0,2:T(2,128)(2,1)}), bf16[2,128,1024]{1,0,2:T(2,128)(2,1)}, u32[]{:S(2)}, u32[]{:S(2)}) async-start(bf16[2,128,1024]{1,0,2:T(2,128)(2,1)} %copy.69), calls=%async_computation.6 | async-start | bytes 1048576 | tf_op jit(solution)/shard_map/all_to_all | solution.py:152
  464.6 19.7 %all-to-all-start.8 = ((bf16[2,1024,128]{2,0,1:T(2,128)(2,1)}), bf16[2,1024,128]{2,0,1:T(2,128)(2,1)}, u32[]{:S(2)}, u32[]{:S(2)}) async-start(bf16[2,1024,128]{2,0,1:T(2,128)(2,1)} %copy.73), calls=%async_computation.8 | async-start | bytes 1048576 | tf_op jit(solution)/shard_map/all_to_all | solution.py:156
  606.9 24.2 %all-to-all-start.9 = ((bf16[2,128,1024]{1,0,2:T(2,128)(2,1)}), bf16[2,128,1024]{1,0,2:T(2,128)(2,1)}, u32[]{:S(2)}, u32[]{:S(2)}) async-start(bf16[2,128,1024]{1,0,2:T(2,128)(2,1)} %copy.75), calls=%async_computation.9 | async-start | bytes 1048576 | tf_op jit(solution)/shard_map/all_to_all | solution.py:235
  631.1 41.5 %all-to-all-start.13 = ((bf16[2,1024,128]{2,0,1:T(2,128)(2,1)}), bf16[2,1024,128]{2,0,1:T(2,128)(2,1)}, u32[]{:S(2)}, u32[]{:S(2)}) async-start(bf16[2,1024,128]{2,0,1:T(2,128)(2,1)} %copy.83), calls=%async_computation.13 | async-start | bytes 1048576 | tf_op jit(solution)/shard_map/all_to_all | solution.py:156
  672.6 20.6 %all-to-all-start.12 = ((bf16[2,1024,128]{2,0,1:T(2,128)(2,1)}), bf16[2,1024,128]{2,0,1:T(2,128)(2,1)}, u32[]{:S(2)}, u32[]{:S(2)}) async-start(bf16[2,1024,128]{2,0,1:T(2,128)(2,1)} %copy.81), calls=%async_computation.12 | async-start | bytes 1048576 | tf_op jit(solution)/shard_map/all_to_all | solution.py:242
  693.2 19.2 %all-to-all-start.11 = ((bf16[2,1024,128]{2,0,1:T(2,128)(2,1)}), bf16[2,1024,128]{2,0,1:T(2,128)(2,1)S(1)}, u32[]{:S(2)}, u32[]{:S(2)}) async-start(bf16[2,1024,128]{2,0,1:T(2,128)(2,1)} %copy.79), calls=%async_computation.11 | async-start | bytes 1048576 | tf_op jit(solution)/shard_map/all_to_all | solution.py:241
  712.4 20.6 %all-to-all-start.10 = ((bf16[2,1024,128]{2,0,1:T(2,128)(2,1)}), bf16[2,1024,128]{2,0,1:T(2,128)(2,1)S(1)}, u32[]{:S(2)}, u32[]{:S(2)}) async-start(bf16[2,1024,128]{2,0,1:T(2,128)(2,1)} %copy.77), calls=%async_computation.10 | async-start | bytes 1048576 | tf_op jit(solution)/shard_map/all_to_all | solution.py:240
  733.0 34.0 %all-to-all-start.7 = ((bf16[2,1024,128]{2,0,1:T(2,128)(2,1)}), bf16[2,1024,128]{2,0,1:T(2,128)(2,1)}, u32[]{:S(2)}, u32[]{:S(2)}) async-start(bf16[2,1024,128]{2,0,1:T(2,128)(2,1)} %copy.71), calls=%async_computation.7 | async-start | bytes 1048576 | tf_op jit(solution)/shard_map/all_to_all | solution.py:156
  767.1 20.7 %all-to-all-start.14 = ((bf16[2,128,1024]{1,0,2:T(2,128)(2,1)}), bf16[2,128,1024]{1,0,2:T(2,128)(2,1)S(1)}, u32[]{:S(2)}, u32[]{:S(2)}) async-start(bf16[2,128,1024]{1,0,2:T(2,128)(2,1)} %copy.85), calls=%async_computation.14 | async-start | bytes 1048576 | tf_op jit(solution)/shard_map/all_to_all | solution.py:235
  823.2 18.8 %all-to-all-start.17 = ((bf16[2,1024,128]{2,0,1:T(2,128)(2,1)}), bf16[2,1024,128]{2,0,1:T(2,128)(2,1)S(1)}, u32[]{:S(2)}, u32[]{:S(2)}) async-start(bf16[2,1024,128]{2,0,1:T(2,128)(2,1)} %copy.91), calls=%async_computation.17 | async-start | bytes 1048576 | tf_op jit(solution)/shard_map/all_to_all | solution.py:242
  842.0 20.5 %all-to-all-start.15 = ((bf16[2,1024,128]{2,0,1:T(2,128)(2,1)}), bf16[2,1024,128]{2,0,1:T(2,128)(2,1)}, u32[]{:S(2)}, u32[]{:S(2)}) async-start(bf16[2,1024,128]{2,0,1:T(2,128)(2,1)} %copy.87), calls=%async_computation.15 | async-start | bytes 1048576 | tf_op jit(solution)/shard_map/all_to_all | solution.py:240
  862.5 20.6 %all-to-all-start.16 = ((bf16[2,1024,128]{2,0,1:T(2,128)(2,1)}), bf16[2,1024,128]{2,0,1:T(2,128)(2,1)S(1)}, u32[]{:S(2)}, u32[]{:S(2)}) async-start(bf16[2,1024,128]{2,0,1:T(2,128)(2,1)} %copy.89), calls=%async_computation.16 | async-start | bytes 1048576 | tf_op jit(solution)/shard_map/all_to_all | solution.py:241
  867.7 147.6 %all-reduce.3.cloned.1.call-start = ((), (), s32[]{:S(2)}) async-start(), calls=%async_computation.26 | async-start | bytes 262144 | tf_op jit(solution)/shard_map/psum | solution.py:38
  (124 other events, 2641.6 us)
Sparse Core Ops, SparseCore 0:
  11.1 72.8 all-gather.16
  85.9 35.3 all-gather.18
  123.2 87.5 all-gather.22
  212.5 87.5 all-gather.20
  301.8 70.1 all-gather.24
  373.7 35.6 all-gather.26
  411.3 87.5 all-gather.28
  500.8 87.6 all-gather.30
  894.6 120.6 all-reduce.2
where the time goes:
time: 1030 us
  waiting for transfers between devices  582 us (57%)
  matrix products  183 us (18%)
  local copies, waits for them, and re-layouts  114 us (11%)
  starting transfers between devices  79.7 us (8%)
  other arithmetic  48.3 us (5%)
  between operations  16 us (2%)
    psum x1, waiting for transfers between devices, sum_adapters(): return lax.psum((down_terms, up_terms), ('dp', 'sp'))  118 us
    all_gather x2, waiting for transfers between devices, fetch_weights(): lax.all_gather(query_key_value_weight[layer_number], 'dp', axis=0, tiled=...  118 us
    all_gather x2, waiting for transfers between devices, fetch_weights(): lax.all_gather(feedforward_out_weight[layer_number], 'dp', axis=0, tiled=...  104 us
    all_gather x2, waiting for transfers between devices, fetch_weights(): lax.all_gather(feedforward_in_weight[layer_number], 'dp', axis=0, tiled=T...  96 us
    all_to_all x4, waiting for transfers between devices, layer_forward(): lax.all_to_all(mixture_h, 'sp', split_axis=1, concat_axis=2, tiled=True)  30 us
    dot_general x2, matrix products, layer_backward(): jnp.einsum('stf,df->std', grad_pre, feedforward_in_weight, preferred_elem...  24.1 us
    all_to_all x2, waiting for transfers between devices, layer_forward(): lax.all_to_all(query_rows, 'sp', split_axis=2, concat_axis=1, tiled=True)  24.1 us
    dot_general x2, matrix products, layer_forward(): jnp.einsum('stf,fd->std', activation, feedforward_out_weight, preferred_e...  23.5 us
  transfers between devices with their start and end apart: 27, of which 20 were waited for; matrix products, arithmetic and copies ran while one was open for 24% of the time, Pallas kernels for 0%

commit v1 on v0

--- a/solution.py
+++ b/solution.py
@@ -1,3 +1,4 @@
+import functools
 from functools import partial
 import math
 import jax
@@ -10,6 +11,36 @@
 ADAPTER_ALPHA = 32.0
 EXACT_PRECISION = lax.Precision.HIGHEST
 MASKED = -1e30
+
+
+def prepare_patch(a0, in_dim, values):
+    mid_arr, z2 = (a0.shape[:in_dim], a0.shape[in_dim + 1 :])
+    wide_out = a0.reshape(*mid_arr, values, -1, *z2)
+    return jnp.moveaxis(wide_out, in_dim, 0)
+
+
+def define_regions_on(point, at_axis):
+    point = jnp.moveaxis(point, 0, at_axis)
+    x_new = point.shape
+    return point.reshape(
+        *x_new[:at_axis], x_new[at_axis] * x_new[at_axis + 1], *x_new[at_axis + 2 :]
+    )
+
+
+def obtain_widths_up(s0, peer_axis, my_tile, vector):
+    s_next, r1 = (jax.lax.axis_size(peer_axis), jax.lax.axis_index(peer_axis))
+    block_now = prepare_patch(s0, my_tile, s_next)
+    sheets = [block_now[r1]]
+    for ii in tuple(range(1, s_next)):
+        big = block_now[(r1 + ii) % s_next]
+        sheets.append(
+            jax.lax.ppermute(big, peer_axis, [(s, (s + ii) % s_next) for s in range(s_next)])
+        )
+    block_now = jnp.stack(sheets, axis=0)[(r1 - jnp.arange(s_next)) % s_next]
+    return define_regions_on(block_now, vector)
+
+
+draft_the_map = functools.partial(obtain_widths_up, peer_axis="sp", my_tile=2, vector=1)
 
 
 def layer_norm(tensor, gains, shifts):
@@ -150,7 +181,7 @@
     queries_h, keys_h, values_h = (
         lax.all_to_all(query_rows, "sp", split_axis=2, concat_axis=1, tiled=True),
         lax.all_to_all(key_rows, "sp", split_axis=2, concat_axis=1, tiled=True),
-        lax.all_to_all(value_rows, "sp", split_axis=2, concat_axis=1, tiled=True),
+        draft_the_map(value_rows),
     )
     mixture_h, log_total = lax.map(slot_forward, (queries_h, keys_h, values_h, document_begin))
     mixture = lax.all_to_all(mixture_h, "sp", split_axis=1, concat_axis=2, tiled=True)

time: 1030 us -> 1030 us (level)
  waiting for transfers between devices: 582 us -> 555 us
  starting transfers between devices: 79.7 us -> 93.7 us
  local copies, waits for them, and re-layouts: 114 us -> 126 us
    all_to_all x2 -> x0, waiting for transfers between devices: 22.2 us -> none  [layer_forward(): lax.all_to_all(value_rows, 'sp', split_axis=2, concat_axis=1, tiled=True)]
    all_to_all x2, waiting for transfers between devices: 24.1 us -> 5.95 us  [layer_forward(): lax.all_to_all(query_rows, 'sp', split_axis=2, concat_axis=1, tiled=True)]
    ppermute x0 -> x14, starting transfers between devices: none -> 17.8 us  [obtain_widths_up(): jax.lax.ppermute(big, peer_axis, [(s, (s + ii) % s_next) for s in range(s...]
    all_gather x2, waiting for transfers between devices: 96 us -> 107 us  [fetch_weights(): lax.all_gather(feedforward_in_weight[layer_number], 'dp', axis=0, tiled=T...]
  transfers between devices with their start and end apart: 27 -> 39, of which waited for: 20 -> 20; matrix products, arithmetic and copies ran while one was open for 24% -> 26% of each run, Pallas kernels for 0% -> 0%
where the time goes in v1:
time: 1030 us; the launch traced here: 1020 us
  waiting for transfers between devices  555 us (54%)
  matrix products  183 us (18%)
  local copies, waits for them, and re-layouts  126 us (12%)
  starting transfers between devices  93.7 us (9%)
  other arithmetic  48.9 us (5%)
  between operations  16 us (2%)
    psum x1, waiting for transfers between devices, sum_adapters(): return lax.psum((down_terms, up_terms), ('dp', 'sp'))  118 us
    all_gather x2, waiting for transfers between devices, fetch_weights(): lax.all_gather(feedforward_out_weight[layer_number], 'dp', axis=0, tiled=...  114 us
    all_gather x2, waiting for transfers between devices, fetch_weights(): lax.all_gather(query_key_value_weight[layer_number], 'dp', axis=0, tiled=...  113 us
    all_gather x2, waiting for transfers between devices, fetch_weights(): lax.all_gather(feedforward_in_weight[layer_number], 'dp', axis=0, tiled=T...  107 us
    all_to_all x4, waiting for transfers between devices, layer_forward(): lax.all_to_all(mixture_h, 'sp', split_axis=1, concat_axis=2, tiled=True)  29.3 us
    dot_general x2, matrix products, layer_backward(): jnp.einsum('stf,df->std', grad_pre, feedforward_in_weight, preferred_elem...  24.1 us
    dot_general x2, matrix products, layer_forward(): jnp.einsum('stf,fd->std', activation, feedforward_out_weight, preferred_e...  23.5 us
  transfers between devices with their start and end apart: 39, of which 20 were waited for; matrix products, arithmetic and copies ran while one was open for 26% of the time, Pallas kernels for 0%

profile of v1, /device:TPU:0, one launch (start us, length us, event | category | flops | bytes accessed | tf_op | source)
XLA Modules:
  0.0 1024.5 jit_solution(18101502161913877222)
XLA Ops:
  29.6 54.6 %all-gather.17.cloned.1.call-done = bf16[1,1024,3072]{2,1,0:T(8,128)(2,1)} async-done(((bf16[1,256,3072]{2,1,0:T(8,128)(2,1)}), bf16[1,1024,3072]{2,1,0:T(8,128)(2,1)}) %all-gather.17.cloned.1.call-update) | async-done | bytes 6291472 | tf_op jit(solution)/shard_map/all_gather | solution.py:61
  113.4 5.4 all-to-all-done
  118.8 5.8 all-to-all-start.1
  126.4 13.5 %all-to-all-done.1 = bf16[2,128,1024]{1,0,2:T(2,128)(2,1)S(1)} async-done(((bf16[2,128,1024]{1,0,2:T(2,128)(2,1)}), bf16[2,128,1024]{1,0,2:T(2,128)(2,1)S(1)}, u32[]{:S(2)}, u32[]{:S(2)}) %all-to-all-start.1) | async-done | bytes 524320 | tf_op jit(solution)/shard_map/all_to_all | solution.py:183
  140.6 12.9 %while.72 = (s32[]{:T(128)}, bf16[2,1024,128]{1,2,0:T(8,128)(2,1)S(1)}, bf16[2,1024,128]{1,2,0:T(8,128)(2,1)S(1)}, s32[2,1024]{1,0:T(2,128)S(1)}, bf16[2,1024,12...) while((s32[]{:T(128)}, bf16[2,1024,128]{1,2,0:T(8,128)(2,1)S(1)}, ...), condition=%wide.region_5.6_spmd, body=%wide.region_2.5_spmd.sunk | while | flops 556922880 | bytes 32575588 | solution.py:186
  159.7 14.0 %all-to-all-done.2 = bf16[2,1024,128]{2,0,1:T(2,128)(2,1)S(1)} async-done(((bf16[2,1024,128]{2,0,1:T(2,128)(2,1)}), bf16[2,1024,128]{2,0,1:T(2,128)(2,1)S(1)}, u32[]{:S(2)}, u32[]{:S(2)}) %all-to-all-start.2) | async-done | bytes 524320 | tf_op jit(solution)/shard_map/all_to_all | solution.py:187
  177.9 32.9 %all-gather.23.cloned.1.call-done = bf16[1,4096,1024]{2,1,0:T(8,128)(2,1)} async-done(((bf16[1,1024,1024]{2,1,0:T(8,128)(2,1)}), bf16[1,4096,1024]{2,1,0:T(8,128)(2,1)}) %all-gather.23.cloned.1.call-update) | async-done | bytes 8388624 | tf_op jit(solution)/shard_map/all_gather | solution.py:64
  210.8 89.3 %all-gather.21.cloned.1.call-done = bf16[1,1024,4096]{2,1,0:T(8,128)(2,1)} async-done(((bf16[1,256,4096]{2,1,0:T(8,128)(2,1)}), bf16[1,1024,4096]{2,1,0:T(8,128)(2,1)}) %all-gather.21.cloned.1.call-update) | async-done | bytes 8388624 | tf_op jit(solution)/shard_map/all_gather | solution.py:63
  300.2 11.5 %fusion.341 = (f32[2,128]{1,0:T(2,128)S(1)}, f32[2,128,1024]{2,1,0:T(8,128)S(1)}) fusion(f32[2,128,1024]{2,1,0:T(8,128)} %copy-done.50, f32[1024]{0:T(1024)S(1)} %bitcast.832, bf16[1,4096,1024]{2,1,0:T(8,128)(2,1)} %all-gather.23.cloned.1.call-done, bf16[1,1024,4096]{2,1,0:T(8,128)(2,1)} %all-gather.21.cloned.1.call-done, f32[4096]{0:T(1024)S(1)} %bitcast.827, ...), kind=kOutput, calls=%fused_computation.482 | convolution fusion | flops 4307550208 | bytes 18906112 | tf_op jit(solution)/shard_map/stf,fd->std/dot_general | solution.py:201
  313.1 58.9 %all-gather.25.cloned.1.call-done = bf16[1,1024,3072]{2,1,0:T(8,128)(2,1)} async-done(((bf16[1,256,3072]{2,1,0:T(8,128)(2,1)}), bf16[1,1024,3072]{2,1,0:T(8,128)(2,1)}) %all-gather.25.cloned.1.call-update) | async-done | bytes 6291472 | tf_op jit(solution)/shard_map/all_gather | solution.py:61
  408.4 5.8 all-to-all-start.4
  434.8 16.5 %while.74 = (s32[]{:T(128)}, bf16[2,1024,128]{1,2,0:T(8,128)(2,1)}, f32[2,2,1024]{2,1,0:T(2,128)S(1)}, bf16[2,1024,128]{1,2,0:T(8,128)(2,1)S(1)}, s32[2,1024]{1,...) while((s32[]{:T(128)}, bf16[2,1024,128]{1,2,0:T(8,128)(2,1)}, ...), condition=%wide.region_19.20_spmd, body=%wide.region_16.19_spmd.sunk | while | flops 556922880 | bytes 36778152 | solution.py:186
  458.0 15.3 %all-to-all-done.6 = bf16[2,1024,128]{2,0,1:T(2,128)(2,1)} async-done(((bf16[2,1024,128]{2,0,1:T(2,128)(2,1)}), bf16[2,1024,128]{2,0,1:T(2,128)(2,1)}, u32[]{:S(2)}, u32[]{:S(2)}) %all-to-all-start.6) | async-done | bytes 524320 | tf_op jit(solution)/shard_map/all_to_all | solution.py:187
  481.4 17.2 %all-gather.29.cloned.1.call-done = bf16[1,1024,4096]{2,1,0:T(8,128)(2,1)} async-done(((bf16[1,256,4096]{2,1,0:T(8,128)(2,1)}), bf16[1,1024,4096]{2,1,0:T(8,128)(2,1)}) %all-gather.29.cloned.1.call-update) | async-done | bytes 8388624 | tf_op jit(solution)/shard_map/all_gather | solution.py:63
  498.6 8.2 fusion.75
  506.7 81.3 %all-gather.31.cloned.1.call-done = bf16[1,4096,1024]{2,1,0:T(8,128)(2,1)} async-done(((bf16[1,1024,1024]{2,1,0:T(8,128)(2,1)}), bf16[1,4096,1024]{2,1,0:T(8,128)(2,1)}) %all-gather.31.cloned.1.call-update) | async-done | bytes 8388624 | tf_op jit(solution)/shard_map/all_gather | solution.py:64
  588.1 12.2 %multiply_reduce_fusion.5 = (f32[2,128]{1,0:T(2,128)S(1)}, f32[2,128,1024]{2,1,0:T(8,128)}) fusion(f32[2,128,1024]{2,1,0:T(8,128)S(1)} %copy-done.22, f32[2,128]{1,0:T(2,128)S(1)} %broadcast_multiply_fusion.5, f32[1024]{0:T(1024)S(1)} %bitcast.841, bf16[1,1024,4096]{2,1,0:T(8,128)(2,1)} %all-gather.29.cloned.1.call-done, f32[2,128,4096]{2,1,0:T(8,128)} %fusion.75, ...), kind=kOutput, calls=%fused_computation.281 | convolution fusion | flops 4316987392 | bytes 23599104 | tf_op jit(solution)/shard_map/stf,df->std/dot_general | solution.py:253
  612.6 15.4 %while.76 = (s32[]{:T(128)}, bf16[2,1024,128]{1,2,0:T(8,128)(2,1)}, f32[2,2,1024]{2,1,0:T(2,128)}, bf16[2,1024,128]{1,2,0:T(8,128)(2,1)S(1)}, s32[2,1024]{1,0:T(...) while((s32[]{:T(128)}, bf16[2,1024,128]{1,2,0:T(8,128)(2,1)}, ...), condition=%wide.region_32.33_spmd, body=%wide.region_29.32_spmd.sunk | while | flops 556922880 | bytes 32583792 | solution.py:186
  630.4 5.3 all-to-all-start.11
  642.6 27.2 %while.75 = (s32[]{:T(128)}, bf16[2,1024,128]{1,2,0:T(8,128)(2,1)}, bf16[2,1024,128]{1,2,0:T(8,128)(2,1)}, bf16[2,1024,128]{1,2,0:T(8,128)(2,1)}, bf16[2,1024,12...) while((s32[]{:T(128)}, bf16[2,1024,128]{1,2,0:T(8,128)(2,1)}, ...), condition=%wide.region_26.27_spmd, body=%wide.region_24.26_spmd.sunk | while | flops 1370880000 | bytes 88150360 | solution.py:267
  684.4 8.0 all-to-all-done.10
  696.2 7.8 fusion.69
  706.0 5.5 all-to-all-done.9
  715.0 12.9 %while.73 = (s32[]{:T(128)}, bf16[2,1024,128]{1,2,0:T(8,128)(2,1)S(1)}, bf16[2,1024,128]{1,2,0:T(8,128)(2,1)S(1)}, s32[2,1024]{1,0:T(2,128)S(1)}, bf16[2,1024,12...) while((s32[]{:T(128)}, bf16[2,1024,128]{1,2,0:T(8,128)(2,1)S(1)}, ...), condition=%wide.region_13.14_spmd, body=%wide.region_10.13_spmd.sunk | while | flops 556922880 | bytes 32575588 | solution.py:186
  732.0 5.5 all-to-all-start.5
  748.2 11.9 %multiply_reduce_fusion.2 = (f32[2,128]{1,0:T(2,128)S(1)}, f32[2,128,1024]{2,1,0:T(8,128)}) fusion(f32[2,128,1024]{2,1,0:T(8,128)S(1)} %copy-done.29, f32[2,128]{1,0:T(2,128)S(1)} %broadcast_multiply_fusion.4, f32[1024]{0:T(1024)S(1)} %bitcast.845, bf16[1,1024,4096]{2,1,0:T(8,128)(2,1)} %all-gather.21.cloned.1.call-done, f32[2,128,4096]{2,1,0:T(8,128)} %fusion.69, ...), kind=kOutput, calls=%fused_computation.275 | convolution fusion | flops 4317249536 | bytes 24123392 | tf_op jit(solution)/shard_map/stf,df->std/dot_general | solution.py:253
  775.9 11.1 %all-to-all-done.12 = bf16[2,128,1024]{1,0,2:T(2,128)(2,1)S(1)} async-done(((bf16[2,128,1024]{1,0,2:T(2,128)(2,1)}), bf16[2,128,1024]{1,0,2:T(2,128)(2,1)S(1)}, u32[]{:S(2)}, u32[]{:S(2)}) %all-to-all-start.12) | async-done | bytes 524320 | tf_op jit(solution)/shard_map/all_to_all | solution.py:266
  791.9 28.5 %while.77 = (s32[]{:T(128)}, bf16[2,1024,128]{1,2,0:T(8,128)(2,1)}, bf16[2,1024,128]{1,2,0:T(8,128)(2,1)}, bf16[2,1024,128]{1,2,0:T(8,128)(2,1)}, bf16[2,1024,12...) while((s32[]{:T(128)}, bf16[2,1024,128]{1,2,0:T(8,128)(2,1)}, ...), condition=%wide.region_39.40_spmd, body=%wide.region_37.39_spmd.sunk | while | flops 1370880000 | bytes 86053176 | solution.py:267
  830.0 11.3 %all-to-all-done.15 = bf16[2,1024,128]{2,0,1:T(2,128)(2,1)S(1)} async-done(((bf16[2,1024,128]{2,0,1:T(2,128)(2,1)}), bf16[2,1024,128]{2,0,1:T(2,128)(2,1)S(1)}, u32[]{:S(2)}, u32[]{:S(2)}) %all-to-all-start.15) | async-done | bytes 524320 | tf_op jit(solution)/shard_map/all_to_all | solution.py:273
  845.8 12.0 %fusion.191 = f32[2,128,1024]{2,1,0:T(8,128)} fusion(f32[2,128,1024]{2,1,0:T(8,128)S(1)} %get-tuple-element.529, bf16[1,4096,1024]{2,1,0:T(8,128)(2,1)} %all-gather.31.cloned.1.call-done, bf16[1,1024,4096]{2,1,0:T(8,128)(2,1)} %all-gather.29.cloned.1.call-done, f32[4096]{0:T(1024)S(1)} %bitcast.826, f32[1024]{0:T(1024)S(1)} %bitcast.829, ...), kind=kOutput, calls=%fused_computation.235 | convolution fusion | flops 4307288064 | bytes 18905088 | tf_op jit(solution)/shard_map/stf,fd->std/dot_general | solution.py:201
  871.0 11.3 %all-to-all-done.14 = bf16[2,1024,128]{2,0,1:T(2,128)(2,1)S(1)} async-done(((bf16[2,1024,128]{2,0,1:T(2,128)(2,1)}), bf16[2,1024,128]{2,0,1:T(2,128)(2,1)S(1)}, u32[]{:S(2)}, u32[]{:S(2)}) %all-to-all-start.14) | async-done | bytes 524320 | tf_op jit(solution)/shard_map/all_to_all | solution.py:272
  896.4 118.3 %all-reduce.3.cloned.1.call-done = (f32[2,2,4,1024]{3,2,1,0:T(4,128)}, f32[2,2,4,1024]{3,2,1,0:T(4,128)}) async-done(((f32[2,2,4,1024]{3,2,1,0:T(4,128)}, f32[2,2,4,1024]{3,2,1,0:T(4,128)}), (f32[2,2,4,1024]{3,2,1,0:T(4,128)}, f32[2,2,4,1024]{3,2,1,0:T(4,128)})) %all-reduce.3.cloned.1.call-update) | async-done | bytes 131088 | tf_op jit(solution)/shard_map/psum | solution.py:69
  (651 shorter events, 373.4 us)
Async XLA Ops:
  7.2 77.0 %all-gather.17.cloned.1.call-start = ((), (), s32[]{:S(2)}) async-start(), calls=%async_computation.16 | async-start | bytes 7864320 | tf_op jit(solution)/shard_map/all_gather | solution.py:61
  11.1 163.9 %all-gather.19.cloned.1.call-start = ((), (), s32[]{:S(2)}) async-start(), calls=%async_computation.17 | async-start | bytes 2621440 | tf_op jit(solution)/shard_map/all_gather | solution.py:62
  12.3 198.5 %all-gather.23.cloned.1.call-start = ((), (), s32[]{:S(2)}) async-start(), calls=%async_computation.19 | async-start | bytes 10485760 | tf_op jit(solution)/shard_map/all_gather | solution.py:64
  17.0 283.2 %all-gather.21.cloned.1.call-start = ((), (), s32[]{:S(2)}) async-start(), calls=%async_computation.18 | async-start | bytes 10485760 | tf_op jit(solution)/shard_map/all_gather | solution.py:63
  21.9 350.1 %all-gather.25.cloned.1.call-start = ((), (), s32[]{:S(2)}) async-start(), calls=%async_computation.20 | async-start | bytes 7864320 | tf_op jit(solution)/shard_map/all_gather | solution.py:61
  22.5 455.0 %all-gather.27.cloned.1.call-start = ((), (), s32[]{:S(2)}) async-start(), calls=%async_computation.21 | async-start | bytes 2621440 | tf_op jit(solution)/shard_map/all_gather | solution.py:62
  23.1 475.5 %all-gather.29.cloned.1.call-start = ((), (), s32[]{:S(2)}) async-start(), calls=%async_computation.22 | async-start | bytes 10485760 | tf_op jit(solution)/shard_map/all_gather | solution.py:63
  23.9 564.2 %all-gather.31.cloned.1.call-start = ((), (), s32[]{:S(2)}) async-start(), calls=%async_computation.23 | async-start | bytes 10485760 | tf_op jit(solution)/shard_map/all_gather | solution.py:64
  92.7 26.1 %all-to-all-start = ((bf16[2,128,1024]{1,0,2:T(2,128)(2,1)}), bf16[2,128,1024]{1,0,2:T(2,128)(2,1)S(1)}, u32[]{:S(2)}, u32[]{:S(2)}) async-start(bf16[2,128,1024]{1,0,2:T(2,128)(2,1)} %copy.156), calls=%async_computation | async-start | bytes 1048576 | tf_op jit(solution)/shard_map/all_to_all | solution.py:182
  104.4 20.2 %collective-permute-start.2 = (bf16[2,128,128]{2,1,0:T(8,128)(2,1)S(1)}, bf16[2,128,128]{2,1,0:T(8,128)(2,1)S(1)}, u32[]{:S(2)}, u32[]{:S(2)}) collective-permute-start(bf16[2,128,128]{2,1,0:T(8,128)(2,1)S(1)} %bitcast.807), channel_id=1, source_target_pairs={{0,3},{1,4},{2,5},{3,6},{4,7},{5,0},{6,1},{7,2},{8,11},{9,12},{10,... | collective-permute-start | bytes 196616 | tf_op jit(solution)/shard_map/ppermute | solution.py:37
  106.7 17.9 %collective-permute-start.3 = (bf16[2,128,128]{2,1,0:T(8,128)(2,1)S(1)}, bf16[2,128,128]{2,1,0:T(8,128)(2,1)S(1)}, u32[]{:S(2)}, u32[]{:S(2)}) collective-permute-start(bf16[2,128,128]{2,1,0:T(8,128)(2,1)S(1)} %bitcast.805), channel_id=1, source_target_pairs={{0,4},{1,5},{2,6},{3,7},{4,0},{5,1},{6,2},{7,3},{8,12},{9,13},{10,... | collective-permute-start | bytes 196616 | tf_op jit(solution)/shard_map/ppermute | solution.py:37
  108.3 16.4 %collective-permute-start.4 = (bf16[2,128,128]{2,1,0:T(8,128)(2,1)S(1)}, bf16[2,128,128]{2,1,0:T(8,128)(2,1)S(1)}, u32[]{:S(2)}, u32[]{:S(2)}) collective-permute-start(bf16[2,128,128]{2,1,0:T(8,128)(2,1)S(1)} %bitcast.803), channel_id=1, source_target_pairs={{0,5},{1,6},{2,7},{3,0},{4,1},{5,2},{6,3},{7,4},{8,13},{9,14},{10,... | collective-permute-start | bytes 196616 | tf_op jit(solution)/shard_map/ppermute | solution.py:37
  118.8 21.1 %all-to-all-start.1 = ((bf16[2,128,1024]{1,0,2:T(2,128)(2,1)}), bf16[2,128,1024]{1,0,2:T(2,128)(2,1)S(1)}, u32[]{:S(2)}, u32[]{:S(2)}) async-start(bf16[2,128,1024]{1,0,2:T(2,128)(2,1)} %copy.158), calls=%async_computation.1 | async-start | bytes 1048576 | tf_op jit(solution)/shard_map/all_to_all | solution.py:183
  154.6 19.1 %all-to-all-start.2 = ((bf16[2,1024,128]{2,0,1:T(2,128)(2,1)}), bf16[2,1024,128]{2,0,1:T(2,128)(2,1)S(1)}, u32[]{:S(2)}, u32[]{:S(2)}) async-start(bf16[2,1024,128]{2,0,1:T(2,128)(2,1)} %copy.161), calls=%async_computation.2 | async-start | bytes 1048576 | tf_op jit(solution)/shard_map/all_to_all | solution.py:187
  382.2 26.3 %all-to-all-start.3 = ((bf16[2,128,1024]{1,0,2:T(2,128)(2,1)}), bf16[2,128,1024]{1,0,2:T(2,128)(2,1)}, u32[]{:S(2)}, u32[]{:S(2)}) async-start(bf16[2,128,1024]{1,0,2:T(2,128)(2,1)} %copy.172), calls=%async_computation.3 | async-start | bytes 1048576 | tf_op jit(solution)/shard_map/all_to_all | solution.py:182
  396.1 18.2 %collective-permute-start.9 = (bf16[2,128,128]{2,1,0:T(8,128)(2,1)S(1)}, bf16[2,128,128]{2,1,0:T(8,128)(2,1)}, u32[]{:S(2)}, u32[]{:S(2)}) collective-permute-start(bf16[2,128,128]{2,1,0:T(8,128)(2,1)S(1)} %bitcast.808), channel_id=1, source_target_pairs={{0,3},{1,4},{2,5},{3,6},{4,7},{5,0},{6,1},{7,2},{8,11},{9,12},{10,... | collective-permute-start | bytes 196616 | tf_op jit(solution)/shard_map/ppermute | solution.py:37
  398.3 17.4 %collective-permute-start.10 = (bf16[2,128,128]{2,1,0:T(8,128)(2,1)S(1)}, bf16[2,128,128]{2,1,0:T(8,128)(2,1)}, u32[]{:S(2)}, u32[]{:S(2)}) collective-permute-start(bf16[2,128,128]{2,1,0:T(8,128)(2,1)S(1)} %bitcast.806), channel_id=1, source_target_pairs={{0,4},{1,5},{2,6},{3,7},{4,0},{5,1},{6,2},{7,3},{8,12},{9,13},{10,... | collective-permute-start | bytes 196616 | tf_op jit(solution)/shard_map/ppermute | solution.py:37
  399.9 17.3 %collective-permute-start.11 = (bf16[2,128,128]{2,1,0:T(8,128)(2,1)S(1)}, bf16[2,128,128]{2,1,0:T(8,128)(2,1)}, u32[]{:S(2)}, u32[]{:S(2)}) collective-permute-start(bf16[2,128,128]{2,1,0:T(8,128)(2,1)S(1)} %bitcast.804), channel_id=1, source_target_pairs={{0,5},{1,6},{2,7},{3,0},{4,1},{5,2},{6,3},{7,4},{8,13},{9,14},{10,... | collective-permute-start | bytes 196616 | tf_op jit(solution)/shard_map/ppermute | solution.py:37
  402.2 16.5 %collective-permute-start.12 = (bf16[2,128,128]{2,1,0:T(8,128)(2,1)S(1)}, bf16[2,128,128]{2,1,0:T(8,128)(2,1)S(1)}, u32[]{:S(2)}, u32[]{:S(2)}) collective-permute-start(bf16[2,128,128]{2,1,0:T(8,128)(2,1)S(1)} %bitcast.802), channel_id=1, source_target_pairs={{0,6},{1,7},{2,0},{3,1},{4,2},{5,3},{6,4},{7,5},{8,14},{9,15},{10,... | collective-permute-start | bytes 196616 | tf_op jit(solution)/shard_map/ppermute | solution.py:37
  408.4 21.3 %all-to-all-start.4 = ((bf16[2,128,1024]{1,0,2:T(2,128)(2,1)}), bf16[2,128,1024]{1,0,2:T(2,128)(2,1)}, u32[]{:S(2)}, u32[]{:S(2)}) async-start(bf16[2,128,1024]{1,0,2:T(2,128)(2,1)} %copy.174), calls=%async_computation.4 | async-start | bytes 1048576 | tf_op jit(solution)/shard_map/all_to_all | solution.py:183
  453.4 19.9 %all-to-all-start.6 = ((bf16[2,1024,128]{2,0,1:T(2,128)(2,1)}), bf16[2,1024,128]{2,0,1:T(2,128)(2,1)}, u32[]{:S(2)}, u32[]{:S(2)}) async-start(bf16[2,1024,128]{2,0,1:T(2,128)(2,1)} %copy.180), calls=%async_computation.6 | async-start | bytes 1048576 | tf_op jit(solution)/shard_map/all_to_all | solution.py:187
  606.5 23.9 %all-to-all-start.7 = ((bf16[2,128,1024]{1,0,2:T(2,128)(2,1)}), bf16[2,128,1024]{1,0,2:T(2,128)(2,1)}, u32[]{:S(2)}, u32[]{:S(2)}) async-start(bf16[2,128,1024]{1,0,2:T(2,128)(2,1)} %copy.182), calls=%async_computation.7 | async-start | bytes 1048576 | tf_op jit(solution)/shard_map/all_to_all | solution.py:266
  630.4 41.5 %all-to-all-start.11 = ((bf16[2,1024,128]{2,0,1:T(2,128)(2,1)}), bf16[2,1024,128]{2,0,1:T(2,128)(2,1)}, u32[]{:S(2)}, u32[]{:S(2)}) async-start(bf16[2,1024,128]{2,0,1:T(2,128)(2,1)} %copy.192), calls=%async_computation.11 | async-start | bytes 1048576 | tf_op jit(solution)/shard_map/all_to_all | solution.py:187
  671.9 20.6 %all-to-all-start.10 = ((bf16[2,1024,128]{2,0,1:T(2,128)(2,1)}), bf16[2,1024,128]{2,0,1:T(2,128)(2,1)}, u32[]{:S(2)}, u32[]{:S(2)}) async-start(bf16[2,1024,128]{2,0,1:T(2,128)(2,1)} %copy.189), calls=%async_computation.10 | async-start | bytes 1048576 | tf_op jit(solution)/shard_map/all_to_all | solution.py:273
  692.5 19.0 %all-to-all-start.9 = ((bf16[2,1024,128]{2,0,1:T(2,128)(2,1)}), bf16[2,1024,128]{2,0,1:T(2,128)(2,1)S(1)}, u32[]{:S(2)}, u32[]{:S(2)}) async-start(bf16[2,1024,128]{2,0,1:T(2,128)(2,1)} %copy.187), calls=%async_computation.9 | async-start | bytes 1048576 | tf_op jit(solution)/shard_map/all_to_all | solution.py:272
  711.4 20.6 %all-to-all-start.8 = ((bf16[2,1024,128]{2,0,1:T(2,128)(2,1)}), bf16[2,1024,128]{2,0,1:T(2,128)(2,1)S(1)}, u32[]{:S(2)}, u32[]{:S(2)}) async-start(bf16[2,1024,128]{2,0,1:T(2,128)(2,1)} %copy.185), calls=%async_computation.8 | async-start | bytes 1048576 | tf_op jit(solution)/shard_map/all_to_all | solution.py:271
  732.0 34.3 %all-to-all-start.5 = ((bf16[2,1024,128]{2,0,1:T(2,128)(2,1)}), bf16[2,1024,128]{2,0,1:T(2,128)(2,1)}, u32[]{:S(2)}, u32[]{:S(2)}) async-start(bf16[2,1024,128]{2,0,1:T(2,128)(2,1)} %copy.177), calls=%async_computation.5 | async-start | bytes 1048576 | tf_op jit(solution)/shard_map/all_to_all | solution.py:187
  766.3 20.6 %all-to-all-start.12 = ((bf16[2,128,1024]{1,0,2:T(2,128)(2,1)}), bf16[2,128,1024]{1,0,2:T(2,128)(2,1)S(1)}, u32[]{:S(2)}, u32[]{:S(2)}) async-start(bf16[2,128,1024]{1,0,2:T(2,128)(2,1)} %copy.194), calls=%async_computation.12 | async-start | bytes 1048576 | tf_op jit(solution)/shard_map/all_to_all | solution.py:266
  822.5 18.8 %all-to-all-start.15 = ((bf16[2,1024,128]{2,0,1:T(2,128)(2,1)}), bf16[2,1024,128]{2,0,1:T(2,128)(2,1)S(1)}, u32[]{:S(2)}, u32[]{:S(2)}) async-start(bf16[2,1024,128]{2,0,1:T(2,128)(2,1)} %copy.201), calls=%async_computation.15 | async-start | bytes 1048576 | tf_op jit(solution)/shard_map/all_to_all | solution.py:273
  841.3 20.5 %all-to-all-start.13 = ((bf16[2,1024,128]{2,0,1:T(2,128)(2,1)}), bf16[2,1024,128]{2,0,1:T(2,128)(2,1)}, u32[]{:S(2)}, u32[]{:S(2)}) async-start(bf16[2,1024,128]{2,0,1:T(2,128)(2,1)} %copy.197), calls=%async_computation.13 | async-start | bytes 1048576 | tf_op jit(solution)/shard_map/all_to_all | solution.py:271
  861.8 20.6 %all-to-all-start.14 = ((bf16[2,1024,128]{2,0,1:T(2,128)(2,1)}), bf16[2,1024,128]{2,0,1:T(2,128)(2,1)S(1)}, u32[]{:S(2)}, u32[]{:S(2)}) async-start(bf16[2,1024,128]{2,0,1:T(2,128)(2,1)} %copy.199), calls=%async_computation.14 | async-start | bytes 1048576 | tf_op jit(solution)/shard_map/all_to_all | solution.py:272
  867.0 147.7 %all-reduce.3.cloned.1.call-start = ((), (), s32[]{:S(2)}) async-start(), calls=%async_computation.24 | async-start | bytes 262144 | tf_op jit(solution)/shard_map/psum | solution.py:69
  (138 other events, 3366.7 us)
Sparse Core Ops, SparseCore 0:
  11.2 72.8 all-gather.16
  86.0 35.3 all-gather.18
  123.2 87.5 all-gather.22
  212.5 87.5 all-gather.20
  301.8 70.1 all-gather.24
  373.7 35.3 all-gather.26
  410.9 87.5 all-gather.28
  500.4 87.5 all-gather.30
  893.9 120.7 all-reduce.2
